TPU v7x, 256 devices: a whole 4x4x8 slice. The times are simulated.
256 devices in a mesh: cand: 32 (over y, z), tp: 8 (over x, core).
Axes of the slice: x: 4, y: 4, z: 8, core: 2. Of those that a mesh axis runs over, the one named last changes fastest.
Arguments:
- reward_query: bfloat16 [256, 32, 8192], P('cand', None, 'tp'), may hold values from -170 to 170
- reward_new: bfloat16 [256, 2, 32, 1024], P('cand', None, None, 'tp'), may hold values from -7 to 7
- reward_key_value_cache: bfloat16 [256, 2, 768, 1024], P('cand', None, None, 'tp'), may hold values from -6 to 6
- reward_length: int32 [256], P('cand'), may hold values from 1 to 768
- out_weight: bfloat16 [8192, 4096], P('tp'), may hold values from -0.09375 to 0.09375
- policy_cache: bfloat16 [256, 2, 768, 1024], P('cand', None, None, 'tp'), may hold values from -6 to 6
- policy_length: int32 [256], replicated, may hold values from 1 to 767
- source: int32 [128], replicated, may hold values from 0 to 255, as said below
- policy_query: bfloat16 [128, 8192], P('cand', 'tp'), may hold values from -170 to 170
- policy_new: bfloat16 [128, 2, 1024], P('cand', None, 'tp'), may hold values from -7 to 7
Outputs:
- reward_out: bfloat16 [8192, 4096], P('cand', 'tp')
- compacted: bfloat16 [128, 2, 768, 1024], P('cand', None, None, 'tp')
- policy_attn: bfloat16 [128, 8192], P('cand', 'tp')
Inputs may be any that keep to these rules, and one draw needn't show every extreme that they name: `source`: distinct candidate indices; the 8 candidates of each index of cand are named exactly 4 times.
All inputs are finite; a program needn't handle non-finite values.
Results may differ from a plain program's by a relative error of at most 0.0057.
Values may be sent and summed in bfloat16 or wider, within the bound.
A program may use at most 128 MiB of HBM per device.

v0:
```python
import jax
import jax.numpy as jnp
from jax import lax
from jax.sharding import PartitionSpec as P

ASKING_UNITS = 64
SHARED_KV_UNITS = 8
ATTN_DIM = 128
NEW_TOKEN_COUNT = 32
CACHE_LENGTH = 768


def body(
    reward_query,
    reward_new,
    reward_key_value_cache,
    reward_length,
    out_weight,
    policy_cache,
    policy_length,
    source,
    policy_query,
    policy_new,
):
    attention_clusters = ASKING_UNITS // SHARED_KV_UNITS
    score_scale = ATTN_DIM ** (-0.5)
    count = reward_query.shape[0]
    kv_heads = reward_key_value_cache.shape[-1] // ATTN_DIM
    head_list = reward_query.reshape(count, NEW_TOKEN_COUNT, kv_heads, attention_clusters, ATTN_DIM)
    cache_keys = reward_key_value_cache[:, 0].reshape(count, CACHE_LENGTH, kv_heads, ATTN_DIM)
    cache_values = reward_key_value_cache[:, 1].reshape(count, CACHE_LENGTH, kv_heads, ATTN_DIM)
    fresh_keys = reward_new[:, 0].reshape(count, NEW_TOKEN_COUNT, kv_heads, ATTN_DIM)
    fresh_values = reward_new[:, 1].reshape(count, NEW_TOKEN_COUNT, kv_heads, ATTN_DIM)
    old_scores = (
        jnp.einsum("ctkgd,cpkd->ckgtp", head_list, cache_keys, preferred_element_type=jnp.float32)
        * score_scale
    )
    new_scores = (
        jnp.einsum("ctkgd,cukd->ckgtu", head_list, fresh_keys, preferred_element_type=jnp.float32)
        * score_scale
    )
    cache_rows = lax.iota(jnp.int32, CACHE_LENGTH)
    old_visible = cache_rows[None, :] < reward_length[:, None]
    old_scores = jnp.where(old_visible[:, None, None, None, :], old_scores, -1e30)
    token_rows = lax.iota(jnp.int32, NEW_TOKEN_COUNT)
    new_visible = token_rows[None, :] <= token_rows[:, None]
    new_scores = jnp.where(new_visible, new_scores, -1e30)
    peak = jnp.maximum(old_scores.max(-1), new_scores.max(-1))[..., None]
    old_exp = jnp.exp(old_scores - peak)
    new_exp = jnp.exp(new_scores - peak)
    denominator = old_exp.sum(-1, keepdims=True) + new_exp.sum(-1, keepdims=True)
    old_weights = (old_exp / denominator).astype(jnp.bfloat16)
    new_weights = (new_exp / denominator).astype(jnp.bfloat16)
    mixed = jnp.einsum(
        "ckgtp,cpkd->ctkgd", old_weights, cache_values, preferred_element_type=jnp.float32
    )
    mixed = mixed + jnp.einsum(
        "ckgtu,cukd->ctkgd", new_weights, fresh_values, preferred_element_type=jnp.float32
    )
    attn_rows = mixed.reshape(
        count * NEW_TOKEN_COUNT, kv_heads * attention_clusters * ATTN_DIM
    ).astype(jnp.bfloat16)
    partial_value = jnp.dot(attn_rows, out_weight, preferred_element_type=jnp.float32)
    reward_out = lax.psum_scatter(partial_value, "tp", scatter_dimension=1, tiled=True).astype(
        jnp.bfloat16
    )
    slot_count = policy_query.shape[0]
    spread = lax.all_to_all(policy_cache, "cand", split_axis=2, concat_axis=0, tiled=True)
    selected = jnp.take(spread, source, axis=0)
    moved = lax.all_to_all(selected, "cand", split_axis=0, concat_axis=2, tiled=True)
    local_source = lax.dynamic_slice_in_dim(source, lax.axis_index("cand") * slot_count, slot_count)
    slot_lengths = jnp.take(policy_length, local_source)
    compacted = jnp.where(
        cache_rows[None, None, :, None] == slot_lengths[:, None, None, None],
        policy_new[:, :, None, :],
        moved,
    )
    slot_heads = policy_query.reshape(slot_count, kv_heads, attention_clusters, ATTN_DIM)
    slot_keys = compacted[:, 0].reshape(slot_count, CACHE_LENGTH, kv_heads, ATTN_DIM)
    slot_values = compacted[:, 1].reshape(slot_count, CACHE_LENGTH, kv_heads, ATTN_DIM)
    slot_scores = (
        jnp.einsum("skgd,spkd->skgp", slot_heads, slot_keys, preferred_element_type=jnp.float32)
        * score_scale
    )
    slot_visible = cache_rows[None, :] <= slot_lengths[:, None]
    slot_scores = jnp.where(slot_visible[:, None, None, :], slot_scores, -1e30)
    slot_weights = jax.nn.softmax(slot_scores, axis=-1).astype(jnp.bfloat16)
    policy_attn = jnp.einsum(
        "skgp,spkd->skgd", slot_weights, slot_values, preferred_element_type=jnp.float32
    )
    policy_attn = policy_attn.reshape(slot_count, kv_heads * attention_clusters * ATTN_DIM).astype(
        jnp.bfloat16
    )
    return (reward_out, compacted, policy_attn)


def solution(mesh):
    in_specs = (
        P("cand", None, "tp"),
        P("cand", None, None, "tp"),
        P("cand", None, None, "tp"),
        P("cand"),
        P("tp", None),
        P("cand", None, None, "tp"),
        P(),
        P(),
        P("cand", "tp"),
        P("cand", None, "tp"),
    )
    out_specs = (P("cand", "tp"), P("cand", None, None, "tp"), P("cand", "tp"))
    return jax.shard_map(body, mesh=mesh, in_specs=in_specs, out_specs=out_specs, check_vma=False)
```

profile of v0, /device:TPU:6, one launch (start us, length us, event | category | flops | bytes accessed | tf_op | source)
XLA Modules:
  0.0 163.3 jit_solution(17396222381493303545)
XLA Ops:
  7.2 0.0 copy-start
  7.2 5.7 %copy.68 = bf16[8,2,768,128]{3,0,1,2:T(8,128)(2,1)} copy(bf16[8,2,768,128]{3,2,1,0:T(8,128)(2,1)} %param.15) | data formatting | bytes 6291456 | tf_op args[5]
  12.9 0.0 copy-start.5
  12.9 11.7 %all-to-all-start = ((bf16[8,2,768,128]{3,0,1,2:T(8,128)(2,1)}), bf16[8,2,768,128]{3,0,1,2:T(8,128)(2,1)}, u32[]{:S(2)}, u32[]{:S(2)}) async-start(bf16[8,2,768,128]{3,0,1,2:T(8,128)(2,1)} %copy.68), calls=%async_computation.1 | async-start | bytes 6291456 | tf_op jit(solution)/shard_map/all_to_all | solution.py:68
  24.6 0.0 reduce-scatter.2.cloned.1.call-start
  24.7 0.0 copy-done.5
  24.7 0.1 iota_compare_fusion
  24.8 0.0 copy-done
  24.8 0.0 copy-start.2
  24.8 2.6 %bitcast_reduce_fusion = (f32[8,8,32]{2,1,0:T(8,128)S(1)}, f32[8,768,32,8]{1,2,3,0:T(8,128)S(1)}) fusion(pred[8,768]{1,0:T(8,128)(4,1)S(1)} %iota_compare_fusion, bf16[8,2,768,128]{3,2,1,0:T(8,128)(2,1)} %param.12, bf16[8,32,1024]{2,1,0:T(8,128)(2,1)S(1)} %copy-done), kind=kOutput, calls=%fused_computation.4 | convolution fusion | flops 407369728 | bytes 8402944 | tf_op jit(solution)/shard_map/ctkgd,cpkd->ckgtp/dot_general | solution.py:35
  27.4 0.0 copy-done.2
  27.4 0.9 fusion.39
  28.3 0.0 copy-start.6
  28.3 1.8 %fusion.2 = f32[8,8,32]{2,1,0:T(8,128)S(1)} fusion(f32[8,768,32,8]{1,2,3,0:T(8,128)S(1)} %get-tuple-element.21, f32[8,8,32]{2,1,0:T(8,128)S(1)} %max.11, pred[8,768]{1,0:T(8,128)(4,1)S(1)} %iota_compare_fusion), kind=kLoop, calls=%fused_computation.8 | loop fusion | flops 6289408 | bytes 6313984 | tf_op jit(solution)/shard_map/reduce_sum | solution.py:51
  30.1 0.0 slice-start
  30.1 0.3 fusion.20
  30.4 0.0 copy-done.6
  30.4 0.0 slice-start.1
  30.4 2.4 %fusion.3 = f32[8,8,32,128]{3,2,1,0:T(8,128)S(1)} fusion(f32[8,768,32,8]{1,2,3,0:T(8,128)S(1)} %get-tuple-element.21, f32[8,8,32]{2,1,0:T(8,128)S(1)} %add.31, f32[8,8,32]{2,1,0:T(8,128)S(1)} %max.11, pred[8,768]{1,0:T(8,128)(4,1)S(1)} %iota_compare_fusion, bf16[8,2,768,128]{3,2,1,0:T(8,128)(2,1)S(1)} %copy-done.6), kind=kOutput, calls=%fused_computation.9 | convolution fusion | flops 410517504 | bytes 8984576 | tf_op jit(solution)/shard_map/ckgtp,cpkd->ctkgd/dot_general | solution.py:54
  32.9 0.4 fusion.14
  33.3 0.2 copy.66
  33.5 0.0 slice-done
  33.5 0.1 slice-done.1
  33.5 4.3 %fusion.21 = f32[256,4096]{1,0:T(8,128)} fusion(bf16[1024,4096]{1,0:T(8,128)(2,1)S(1)} %bitcast.135, bf16[32,8,8,128]{3,2,1,0:T(8,128)(2,1)S(1)} %bitcast.138), kind=kOutput, calls=%fused_computation.37 | convolution fusion | flops 2147483648 | bytes 13107200 | tf_op jit(solution)/shard_map/dot_general | solution.py:63
  37.9 0.0 copy-start.4
  37.9 0.0 reduce-scatter.2.cloned.1.call-update
  37.9 0.6 copy-done.4
  38.6 60.7 %all-to-all-done = bf16[8,2,768,128]{3,0,1,2:T(8,128)(2,1)} async-done(((bf16[8,2,768,128]{3,0,1,2:T(8,128)(2,1)}), bf16[8,2,768,128]{3,0,1,2:T(8,128)(2,1)}, u32[]{:S(2)}, u32[]{:S(2)}) %all-to-all-start) | async-done | bytes 3145760 | tf_op jit(solution)/shard_map/all_to_all | solution.py:68
  99.3 4.4 %copy.70 = bf16[32,8,2,24,128]{4,3,2,1,0:T(8,128)(2,1)} copy(bf16[32,8,2,24,128]{4,1,2,3,0:T(8,128)(2,1)} %bitcast.23) | data formatting | bytes 6291456 | tf_op jit(solution)/shard_map/all_to_all | solution.py:68
  103.7 2.7 %gather_fusion.1 = bf16[128,2,24,128]{3,2,1,0:T(8,128)(2,1)S(1)} fusion(bf16[256,2,24,128]{3,2,1,0:T(8,128)(2,1)} %bitcast.136, s32[1024]{0:T(1024)S(1)} %pad_clamp_fusion), kind=kCustom, calls=%fused_computation.1 | custom fusion | bytes 3146240 | tf_op jit(solution)/shard_map/jit(_take)/gather | solution.py:69
  106.4 0.0 copy-start.3
  106.4 0.0 copy-start.1
  106.5 1.4 broadcast_select_fusion
  107.8 5.8 %all-to-all-start.1 = ((bf16[128,2,24,128]{3,2,1,0:T(8,128)(2,1)}), bf16[128,2,24,128]{3,2,1,0:T(8,128)(2,1)S(1)}, u32[]{:S(2)}, u32[]{:S(2)}) async-start(bf16[128,2,24,128]{3,2,1,0:T(8,128)(2,1)} %broadcast_select_fusion), calls=%async_computation.2 | async-start | bytes 3145728 | tf_op jit(solution)/shard_map/all_to_all | solution.py:70
  113.6 0.0 copy-done.3
  113.6 0.1 compare_select_fusion.1
  113.7 0.0 copy-done.1
  113.7 0.6 gather_fusion
  114.4 0.1 and_select_fusion
  114.4 0.1 iota_compare_fusion.2
  114.5 0.0 reduce-scatter.2.cloned.1.call-done
  114.5 1.8 %convert_element_type.41 = bf16[256,512]{1,0:T(8,128)(2,1)} convert(f32[256,512]{1,0:T(8,128)} %reduce-scatter.2.cloned.1.call-done) | non-fusion elementwise | flops 131072 | bytes 786432 | tf_op jit(solution)/shard_map/convert_element_type | solution.py:64
  116.3 36.5 %all-to-all-done.1 = bf16[128,2,24,128]{3,2,1,0:T(8,128)(2,1)S(1)} async-done(((bf16[128,2,24,128]{3,2,1,0:T(8,128)(2,1)}), bf16[128,2,24,128]{3,2,1,0:T(8,128)(2,1)S(1)}, u32[]{:S(2)}, u32[]{:S(2)}) %all-to-all-start.1) | async-done | bytes 1572896 | tf_op jit(solution)/shard_map/all_to_all | solution.py:70
  152.8 0.3 copy.71
  153.1 0.0 copy-start.7
  153.1 0.7 bitcast_select_fusion.1
  153.9 1.3 copy.72
  155.1 0.0 copy-done.7
  155.1 0.5 fusion.40
  155.6 0.3 fusion.19
  155.9 0.6 copy.110
  (9 shorter events, 0.1 us)
Async XLA Ops:
  7.2 17.6 %copy-start = (bf16[8,32,1024]{2,1,0:T(8,128)(2,1)S(1)}, bf16[8,32,1024]{2,1,0:T(8,128)(2,1)}, u32[]{:S(2)}) copy-start(bf16[8,32,1024]{2,1,0:T(8,128)(2,1)} %param.10) | copy-start | bytes 1572868
  12.9 11.8 %copy-start.5 = (s32[8]{0:T(128)S(1)}, s32[8]{0:T(128)}, u32[]{:S(2)}) copy-start(s32[8]{0:T(128)} %param.13) | copy-start | bytes 100
  12.9 86.4 %all-to-all-start = ((bf16[8,2,768,128]{3,0,1,2:T(8,128)(2,1)}), bf16[8,2,768,128]{3,0,1,2:T(8,128)(2,1)}, u32[]{:S(2)}, u32[]{:S(2)}) async-start(bf16[8,2,768,128]{3,0,1,2:T(8,128)(2,1)} %copy.68), calls=%async_computation.1 | async-start | bytes 6291456 | tf_op jit(solution)/shard_map/all_to_all | solution.py:68
  24.6 89.9 %reduce-scatter.2.cloned.1.call-start = ((), (), s32[]{:S(2)}) async-start(), calls=%async_computation.3 | async-start | bytes 4718592 | tf_op jit(solution)/shard_map/reduce_scatter | solution.py:64
  24.8 2.6 %copy-start.2 = (bf16[8,2,32,128]{3,2,1,0:T(8,128)(2,1)S(1)}, bf16[8,2,32,128]{3,2,1,0:T(8,128)(2,1)}, u32[]{:S(2)}) copy-start(bf16[8,2,32,128]{3,2,1,0:T(8,128)(2,1)} %param.11) | copy-start | bytes 393220
  28.3 2.1 %copy-start.6 = (bf16[8,2,768,128]{3,2,1,0:T(8,128)(2,1)S(1)}, bf16[8,2,768,128]{3,2,1,0:T(8,128)(2,1)}, u32[]{:S(2)}) copy-start(bf16[8,2,768,128]{3,2,1,0:T(8,128)(2,1)} %param.12) | copy-start | bytes 9437188
  30.1 3.4 %slice-start = ((s8[8388608]{0:T(1024)(128)(4,1)}), s8[4194304]{0:T(1024)(128)(4,1)S(1)}, s32[]{:S(2)}) async-start(s8[8388608]{0:T(1024)(128)(4,1)} %bitcast.134), calls=%async_computation.4 | async-start | bytes 8388608
  30.4 3.1 %slice-start.1 = ((s8[8388608]{0:T(1024)(128)(4,1)}), s8[4194304]{0:T(1024)(128)(4,1)S(1)}, s32[]{:S(2)}) async-start(s8[8388608]{0:T(1024)(128)(4,1)} %bitcast.134), calls=%async_computation.5 | async-start | bytes 8388608
  37.9 0.7 copy-start.4
  106.4 7.2 %copy-start.3 = (bf16[4,2,128]{2,1,0:T(2,128)(2,1)S(1)}, bf16[4,2,128]{2,1,0:T(2,128)(2,1)}, u32[]{:S(2)}) copy-start(bf16[4,2,128]{2,1,0:T(2,128)(2,1)} %param.19) | copy-start | bytes 6148
  106.4 7.3 %copy-start.1 = (s32[256]{0:T(256)S(1)}, s32[256]{0:T(256)}, u32[]{:S(2)}) copy-start(s32[256]{0:T(256)} %param.16) | copy-start | bytes 3076
  107.8 45.0 %all-to-all-start.1 = ((bf16[128,2,24,128]{3,2,1,0:T(8,128)(2,1)}), bf16[128,2,24,128]{3,2,1,0:T(8,128)(2,1)S(1)}, u32[]{:S(2)}, u32[]{:S(2)}) async-start(bf16[128,2,24,128]{3,2,1,0:T(8,128)(2,1)} %broadcast_select_fusion), calls=%async_computation.2 | async-start | bytes 3145728 | tf_op jit(solution)/shard_map/all_to_all | solution.py:70
  153.1 2.0 %copy-start.7 = (bf16[4,1024]{1,0:T(4,128)(2,1)S(1)}, bf16[4,1024]{1,0:T(4,128)(2,1)}, u32[]{:S(2)}) copy-start(bf16[4,1024]{1,0:T(4,128)(2,1)} %param.18) | copy-start | bytes 24580
Sparse Core Ops, SparseCore 0:
  38.0 38.7 reduce-scatter.1
where the time goes:
time: 164 us; the launch traced here: 163 us
  waiting for transfers between devices  97.3 us (59%)
  starting transfers between devices  17.5 us (11%)
  local copies, waits for them, and re-layouts  16.6 us (10%)
  between operations  14.3 us (9%)
  matrix products  11.4 us (7%)
  other arithmetic  6.26 us (4%)
    all_to_all x1, waiting for transfers between devices, body(): lax.all_to_all(policy_cache, 'cand', split_axis=2, concat_axis=0, tiled=T...  60.7 us
    all_to_all x1, waiting for transfers between devices, body(): lax.all_to_all(selected, 'cand', split_axis=0, concat_axis=2, tiled=True)  36.5 us
    all_to_all x1, starting transfers between devices, body(): lax.all_to_all(policy_cache, 'cand', split_axis=2, concat_axis=0, tiled=T...  11.7 us
    unnamed x24, local copies, waits for them, and re-layouts  8.31 us
    all_to_all x1, starting transfers between devices, body(): lax.all_to_all(selected, 'cand', split_axis=0, concat_axis=2, tiled=True)  5.77 us
    all_to_all x1, local copies, waits for them, and re-layouts, body(): lax.all_to_all(policy_cache, 'cand', split_axis=2, concat_axis=0, tiled=T...  4.41 us
    dot_general x1, matrix products, body(): jnp.dot(attn_rows, out_weight, preferred_element_type=jnp.float32)  4.33 us
  transfers between devices with their start and end apart: 3, of which 2 were waited for; matrix products, arithmetic and copies ran while one was open for 15% of the time, Pallas kernels for 0%

commit v1 on v0

--- a/solution.py
+++ b/solution.py
@@ -67,7 +67,10 @@
     slot_count = policy_query.shape[0]
     spread = lax.all_to_all(policy_cache, "cand", split_axis=2, concat_axis=0, tiled=True)
     selected = jnp.take(spread, source, axis=0)
-    moved = lax.all_to_all(selected, "cand", split_axis=0, concat_axis=2, tiled=True)
+    moved = jnp.concatenate(
+        lax.all_to_all(jnp.stack(jnp.split(selected, lax.axis_size("cand"), axis=0)), "cand", 0, 0),
+        axis=2,
+    )
     local_source = lax.dynamic_slice_in_dim(source, lax.axis_index("cand") * slot_count, slot_count)
     slot_lengths = jnp.take(policy_length, local_source)
     compacted = jnp.where(

time: 164 us -> 183 us (1.12)
  local copies, waits for them, and re-layouts: 16.6 us -> 36.5 us
    unnamed x24 -> x55, local copies, waits for them, and re-layouts: 8.31 us -> 27.6 us
  transfers between devices with their start and end apart: 3 -> 3, of which waited for: 2 -> 2; matrix products, arithmetic and copies ran while one was open for 15% -> 24% of each run, Pallas kernels for 0% -> 0%
where the time goes in v1:
time: 183 us; the launch traced here: 182 us
  waiting for transfers between devices  97.4 us (53%)
  local copies, waits for them, and re-layouts  36.5 us (20%)
  starting transfers between devices  17.7 us (10%)
  between operations  14.3 us (8%)
  matrix products  11.4 us (6%)
  other arithmetic  5.11 us (3%)
    all_to_all x1, waiting for transfers between devices, body(): lax.all_to_all(policy_cache, 'cand', split_axis=2, concat_axis=0, tiled=T...  60.8 us
    all_to_all x1, waiting for transfers between devices, body(): lax.all_to_all(jnp.stack(jnp.split(selected, lax.axis_size('cand'), axis=...  36.5 us
    unnamed x55, local copies, waits for them, and re-layouts  27.6 us
    all_to_all x1, starting transfers between devices, body(): lax.all_to_all(policy_cache, 'cand', split_axis=2, concat_axis=0, tiled=T...  11.7 us
    all_to_all x1, starting transfers between devices, body(): lax.all_to_all(jnp.stack(jnp.split(selected, lax.axis_size('cand'), axis=...  5.9 us
    all_to_all x1, local copies, waits for them, and re-layouts, body(): lax.all_to_all(policy_cache, 'cand', split_axis=2, concat_axis=0, tiled=T...  4.41 us
    dot_general x1, matrix products, body(): jnp.dot(attn_rows, out_weight, preferred_element_type=jnp.float32)  4.34 us
  transfers between devices with their start and end apart: 3, of which 2 were waited for; matrix products, arithmetic and copies ran while one was open for 24% of the time, Pallas kernels for 0%

profile of v1, /device:TPU:6, one launch (start us, length us, event | category | flops | bytes accessed | tf_op | source)
XLA Modules:
  0.0 182.3 jit_solution(1001211189278274659)
XLA Ops:
  7.2 5.7 %copy.99 = bf16[8,2,768,128]{3,0,1,2:T(8,128)(2,1)} copy(bf16[8,2,768,128]{3,2,1,0:T(8,128)(2,1)} %param.15) | data formatting | bytes 6291456 | tf_op args[5]
  12.9 11.7 %all-to-all-start = ((bf16[8,2,768,128]{3,0,1,2:T(8,128)(2,1)}), bf16[8,2,768,128]{3,0,1,2:T(8,128)(2,1)}, u32[]{:S(2)}, u32[]{:S(2)}) async-start(bf16[8,2,768,128]{3,0,1,2:T(8,128)(2,1)} %copy.99), calls=%async_computation.1 | async-start | bytes 6291456 | tf_op jit(solution)/shard_map/all_to_all | solution.py:68
  24.6 0.0 reduce-scatter.2.cloned.1.call-start
  24.7 0.1 iota_compare_fusion
  24.8 0.9 fusion.39
  25.7 2.6 %bitcast_reduce_fusion = (f32[8,8,32]{2,1,0:T(8,128)S(1)}, f32[8,768,32,8]{1,2,3,0:T(8,128)S(1)}) fusion(pred[8,768]{1,0:T(8,128)(4,1)S(1)} %iota_compare_fusion, bf16[8,2,768,128]{3,2,1,0:T(8,128)(2,1)} %param.12, bf16[8,32,1024]{2,1,0:T(8,128)(2,1)S(1)} %copy-done), kind=kOutput, calls=%fused_computation.4 | convolution fusion | flops 407369728 | bytes 8402944 | tf_op jit(solution)/shard_map/ctkgd,cpkd->ckgtp/dot_general | solution.py:35
  28.3 0.3 fusion.20
  28.6 1.8 fusion.2
  30.4 2.4 %fusion.3 = f32[8,8,32,128]{3,2,1,0:T(8,128)S(1)} fusion(f32[8,768,32,8]{1,2,3,0:T(8,128)S(1)} %get-tuple-element.21, f32[8,8,32]{2,1,0:T(8,128)S(1)} %add.31, f32[8,8,32]{2,1,0:T(8,128)S(1)} %max.11, pred[8,768]{1,0:T(8,128)(4,1)S(1)} %iota_compare_fusion, bf16[8,2,768,128]{3,2,1,0:T(8,128)(2,1)S(1)} %copy-done.6), kind=kOutput, calls=%fused_computation.9 | convolution fusion | flops 410517504 | bytes 8984576 | tf_op jit(solution)/shard_map/ckgtp,cpkd->ctkgd/dot_general | solution.py:54
  32.8 0.4 fusion.14
  33.2 0.2 copy.97
  33.5 4.3 %fusion.21 = f32[256,4096]{1,0:T(8,128)} fusion(bf16[1024,4096]{1,0:T(8,128)(2,1)S(1)} %bitcast.261, bf16[32,8,8,128]{3,2,1,0:T(8,128)(2,1)S(1)} %bitcast.264), kind=kOutput, calls=%fused_computation.37 | convolution fusion | flops 2147483648 | bytes 13107200 | tf_op jit(solution)/shard_map/dot_general | solution.py:63
  37.8 0.0 reduce-scatter.2.cloned.1.call-update
  37.8 0.6 copy-done.4
  38.5 60.8 %all-to-all-done = bf16[8,2,768,128]{3,0,1,2:T(8,128)(2,1)} async-done(((bf16[8,2,768,128]{3,0,1,2:T(8,128)(2,1)}), bf16[8,2,768,128]{3,0,1,2:T(8,128)(2,1)}, u32[]{:S(2)}, u32[]{:S(2)}) %all-to-all-start) | async-done | bytes 3145760 | tf_op jit(solution)/shard_map/all_to_all | solution.py:68
  99.3 4.4 %copy.101 = bf16[32,8,2,24,128]{4,3,2,1,0:T(8,128)(2,1)} copy(bf16[32,8,2,24,128]{4,1,2,3,0:T(8,128)(2,1)} %bitcast.23) | data formatting | bytes 6291456 | tf_op jit(solution)/shard_map/all_to_all | solution.py:68
  103.7 2.7 %gather_fusion.1 = bf16[128,2,24,128]{3,2,1,0:T(8,128)(2,1)S(1)} fusion(bf16[256,2,24,128]{3,2,1,0:T(8,128)(2,1)} %bitcast.262, s32[1024]{0:T(1024)S(1)} %pad_clamp_fusion), kind=kCustom, calls=%fused_computation.1 | custom fusion | bytes 3146240 | tf_op jit(solution)/shard_map/jit(_take)/gather | solution.py:69
  106.4 0.2 broadcast_select_fusion
  106.7 0.6 constant_dynamic-update-slice_fusion.31
  107.3 0.6 constant_dynamic-update-slice_fusion.30
  107.9 0.6 constant_dynamic-update-slice_fusion.29
  108.5 0.6 constant_dynamic-update-slice_fusion.28
  109.2 0.6 constant_dynamic-update-slice_fusion.27
  109.8 0.6 constant_dynamic-update-slice_fusion.26
  110.4 0.6 constant_dynamic-update-slice_fusion.25
  111.0 0.6 constant_dynamic-update-slice_fusion.24
  111.7 0.6 constant_dynamic-update-slice_fusion.23
  112.3 0.6 constant_dynamic-update-slice_fusion.22
  112.9 0.6 constant_dynamic-update-slice_fusion.21
  113.5 0.6 constant_dynamic-update-slice_fusion.20
  114.2 0.6 constant_dynamic-update-slice_fusion.19
  114.8 0.6 constant_dynamic-update-slice_fusion.18
  115.4 0.6 constant_dynamic-update-slice_fusion.17
  116.0 0.6 constant_dynamic-update-slice_fusion.16
  116.7 0.6 constant_dynamic-update-slice_fusion.15
  117.3 0.6 constant_dynamic-update-slice_fusion.14
  117.9 0.6 constant_dynamic-update-slice_fusion.13
  118.5 0.6 constant_dynamic-update-slice_fusion.12
  119.2 0.6 constant_dynamic-update-slice_fusion.11
  119.8 0.6 constant_dynamic-update-slice_fusion.10
  120.4 0.6 constant_dynamic-update-slice_fusion.9
  121.0 0.6 constant_dynamic-update-slice_fusion.8
  121.7 0.6 constant_dynamic-update-slice_fusion.7
  122.3 0.6 constant_dynamic-update-slice_fusion.6
  122.9 0.6 constant_dynamic-update-slice_fusion.5
  123.5 0.6 constant_dynamic-update-slice_fusion.4
  124.2 0.6 constant_dynamic-update-slice_fusion.3
  124.8 0.6 constant_dynamic-update-slice_fusion.2
  125.4 0.6 constant_dynamic-update-slice_fusion.1
  126.0 0.6 constant_dynamic-update-slice_fusion
  126.7 5.9 %all-to-all-start.1 = ((bf16[32,4,2,24,128]{4,3,2,1,0:T(8,128)(2,1)}), bf16[32,4,2,24,128]{4,3,2,1,0:T(8,128)(2,1)S(1)}, u32[]{:S(2)}, u32[]{:S(2)}) async-start(bf16[32,4,2,24,128]{4,3,2,1,0:T(8,128)(2,1)} %constant_dynamic-update-slice_fusion), calls=%async_computation.2 | async-start | bytes 3145728 | tf_op jit(solution)/shard_map/all_to_all | solution.py:71
  132.6 0.1 compare_select_fusion.1
  132.7 0.6 gather_fusion
  133.3 0.1 and_select_fusion
  133.4 0.1 iota_compare_fusion.2
  133.5 0.0 reduce-scatter.2.cloned.1.call-done
  133.5 1.8 convert_element_type.41
  135.3 36.5 %all-to-all-done.1 = bf16[32,4,2,24,128]{4,3,2,1,0:T(8,128)(2,1)S(1)} async-done(((bf16[32,4,2,24,128]{4,3,2,1,0:T(8,128)(2,1)}), bf16[32,4,2,24,128]{4,3,2,1,0:T(8,128)(2,1)S(1)}, u32[]{:S(2)}, u32[]{:S(2)}) %all-to-all-start.1) | async-done | bytes 1572896 | tf_op jit(solution)/shard_map/all_to_all | solution.py:71
  171.8 0.3 copy.102
  172.1 0.7 bitcast_select_fusion.1
  172.8 1.3 copy.103
  174.1 0.5 fusion.40
  174.6 0.3 fusion.19
  174.9 0.6 copy.141
  (28 shorter events, 0.1 us)
Async XLA Ops:
  7.2 17.6 %copy-start = (bf16[8,32,1024]{2,1,0:T(8,128)(2,1)S(1)}, bf16[8,32,1024]{2,1,0:T(8,128)(2,1)}, u32[]{:S(2)}) copy-start(bf16[8,32,1024]{2,1,0:T(8,128)(2,1)} %param.10) | copy-start | bytes 1572868
  12.9 11.8 %copy-start.5 = (s32[8]{0:T(128)S(1)}, s32[8]{0:T(128)}, u32[]{:S(2)}) copy-start(s32[8]{0:T(128)} %param.13) | copy-start | bytes 100
  12.9 11.9 %copy-start.2 = (bf16[8,2,32,128]{3,2,1,0:T(8,128)(2,1)S(1)}, bf16[8,2,32,128]{3,2,1,0:T(8,128)(2,1)}, u32[]{:S(2)}) copy-start(bf16[8,2,32,128]{3,2,1,0:T(8,128)(2,1)} %param.11) | copy-start | bytes 393220
  12.9 86.4 %all-to-all-start = ((bf16[8,2,768,128]{3,0,1,2:T(8,128)(2,1)}), bf16[8,2,768,128]{3,0,1,2:T(8,128)(2,1)}, u32[]{:S(2)}, u32[]{:S(2)}) async-start(bf16[8,2,768,128]{3,0,1,2:T(8,128)(2,1)} %copy.99), calls=%async_computation.1 | async-start | bytes 6291456 | tf_op jit(solution)/shard_map/all_to_all | solution.py:68
  24.6 108.9 %reduce-scatter.2.cloned.1.call-start = ((), (), s32[]{:S(2)}) async-start(), calls=%async_computation.3 | async-start | bytes 4718592 | tf_op jit(solution)/shard_map/reduce_scatter | solution.py:64
  28.3 2.1 %copy-start.6 = (bf16[8,2,768,128]{3,2,1,0:T(8,128)(2,1)S(1)}, bf16[8,2,768,128]{3,2,1,0:T(8,128)(2,1)}, u32[]{:S(2)}) copy-start(bf16[8,2,768,128]{3,2,1,0:T(8,128)(2,1)} %param.12) | copy-start | bytes 9437188
  28.6 4.9 %slice-start = ((s8[8388608]{0:T(1024)(128)(4,1)}), s8[4194304]{0:T(1024)(128)(4,1)S(1)}, s32[]{:S(2)}) async-start(s8[8388608]{0:T(1024)(128)(4,1)} %bitcast.260), calls=%async_computation.4 | async-start | bytes 8388608
  30.4 3.1 %slice-start.1 = ((s8[8388608]{0:T(1024)(128)(4,1)}), s8[4194304]{0:T(1024)(128)(4,1)S(1)}, s32[]{:S(2)}) async-start(s8[8388608]{0:T(1024)(128)(4,1)} %bitcast.260), calls=%async_computation.5 | async-start | bytes 8388608
  37.8 0.7 copy-start.4
  126.7 5.9 %copy-start.3 = (bf16[4,2,128]{2,1,0:T(2,128)(2,1)S(1)}, bf16[4,2,128]{2,1,0:T(2,128)(2,1)}, u32[]{:S(2)}) copy-start(bf16[4,2,128]{2,1,0:T(2,128)(2,1)} %param.19) | copy-start | bytes 6148
  126.7 6.0 %copy-start.1 = (s32[256]{0:T(256)S(1)}, s32[256]{0:T(256)}, u32[]{:S(2)}) copy-start(s32[256]{0:T(256)} %param.16) | copy-start | bytes 3076
  126.7 45.2 %all-to-all-start.1 = ((bf16[32,4,2,24,128]{4,3,2,1,0:T(8,128)(2,1)}), bf16[32,4,2,24,128]{4,3,2,1,0:T(8,128)(2,1)S(1)}, u32[]{:S(2)}, u32[]{:S(2)}) async-start(bf16[32,4,2,24,128]{4,3,2,1,0:T(8,128)(2,1)} %constant_dynamic-update-slice_fusion), calls=%async_computation.2 | async-start | bytes 3145728 | tf_op jit(solution)/shard_map/all_to_all | solution.py:71
  172.8 1.3 copy-start.7
Sparse Core Ops, SparseCore 0:
  37.9 38.8 reduce-scatter.1
